TPU v7x, 32 devices: a whole 2x2x4 slice. The times are simulated.
32 devices in a mesh: row: 4 (over x, core), col: 8 (over z, y).
Axes of the slice: x: 2, y: 2, z: 4, core: 2. Of those that a mesh axis runs over, the one named last changes fastest.
Arguments:
- pool: bfloat16 [2048, 1024], P(('row', 'col')), may hold values from -16 to 16
- targets: bfloat16 [2048, 1024], P(('row', 'col')), may hold values from -16 to 16
- counts: int32 [2048], P(('row', 'col')), may hold values from 0 to 7, as said below
Outputs:
- proof: float32 [2048], P(('row', 'col'))
- gradient: float32 [2048, 1024], P(('row', 'col'))
Inputs may be any that keep to these rules, and one draw needn't show every extreme that they name: `counts`: counts of selections; the last pool example has count 7.
All inputs are finite; a program needn't handle non-finite values.
Results may differ from a plain program's by a relative error of at most 0.0014.
Values may be sent and summed in bfloat16 or wider, within the bound.
A program may use at most 64 MiB of HBM per device.

v0:
```python
import jax
import jax.numpy as jnp
from jax import lax
from jax.sharding import PartitionSpec as P


def kernel_tile(row_panel, row_norms, columns):
    col_float = columns.astype(jnp.float32)
    col_norms = jnp.sum(col_float * col_float, axis=1)
    inner = lax.dot_general(
        row_panel, columns, (((1,), (1,)), ((), ())), preferred_element_type=jnp.float32
    )
    squared = row_norms[:, None] + col_norms[None, :] - 2.0 * inner
    return jnp.exp(-squared * (0.5 / columns.shape[1]))


def make_update(row_panel, row_norms):

    def update(totals, pieces, offset):
        col_pool, col_counts, col_targets = pieces
        pool_kernel = (
            kernel_tile(row_panel, row_norms, col_pool) * col_counts.astype(jnp.float32)[None, :]
        )
        target_kernel = kernel_tile(row_panel, row_norms, col_targets)
        pool_mass = jnp.sum(pool_kernel, axis=1)
        target_mass = jnp.sum(target_kernel, axis=1)
        pool_pull = jnp.dot(
            pool_kernel.astype(jnp.bfloat16), col_pool, preferred_element_type=jnp.float32
        )
        target_pull = jnp.dot(
            target_kernel.astype(jnp.bfloat16), col_targets, preferred_element_type=jnp.float32
        )
        return (pool_mass, target_mass, pool_pull, target_pull)

    return update


def finish(row_panel, totals, weight_total, target_count):
    row_float = row_panel.astype(jnp.float32)
    pool_mass, target_mass, pool_pull, target_pull = totals
    proof = target_mass / target_count - pool_mass / weight_total
    gradient = (target_pull - target_mass[:, None] * row_float) / target_count - (
        pool_pull - pool_mass[:, None] * row_float
    ) / weight_total
    return (proof, gradient)


def on_device(pool, targets, counts):
    weight_total = lax.psum(jnp.sum(counts.astype(jnp.float32)), ("row", "col"))
    target_count = targets.shape[0] * lax.axis_size("row") * lax.axis_size("col")
    row_panel = lax.all_gather(pool, "row", axis=0, tiled=True)
    row_float = row_panel.astype(jnp.float32)
    row_norms = jnp.sum(row_float * row_float, axis=1)
    panel_size = row_panel.shape[0]
    width = row_panel.shape[1]
    initial = (
        jnp.zeros((panel_size,), jnp.float32),
        jnp.zeros((panel_size,), jnp.float32),
        jnp.zeros((panel_size, width), jnp.float32),
        jnp.zeros((panel_size, width), jnp.float32),
    )
    update = make_update(row_panel, row_norms)
    totals = update(
        initial,
        (
            lax.all_gather(pool, "col", axis=0, tiled=True),
            lax.all_gather(counts, "col", axis=0, tiled=True),
            lax.all_gather(targets, "col", axis=0, tiled=True),
        ),
        jnp.int32(0),
    )
    proof, gradient = finish(row_panel, totals, weight_total, target_count)
    proof, gradient = (
        lax.psum_scatter(proof, "row", scatter_dimension=0, tiled=True),
        lax.psum_scatter(gradient, "row", scatter_dimension=0, tiled=True),
    )
    return (proof, gradient)


def solution(mesh):
    in_specs = (P(("row", "col"), None), P(("row", "col"), None), P(("row", "col")))
    out_specs = (P(("row", "col")), P(("row", "col"), None))
    return jax.shard_map(
        on_device, mesh=mesh, in_specs=in_specs, out_specs=out_specs, check_vma=False
    )
```

profile of v0, /device:TPU:0, one launch (start us, length us, event | category | flops | bytes accessed | tf_op | source)
XLA Modules:
  0.0 130.5 jit_solution(14796114547563036082)
XLA Ops:
  7.2 0.7 all-gather.3.cloned.1.call-update
  7.9 0.7 all-gather.5.cloned.1.call-update
  8.6 0.0 reduce-scatter.2.cloned.1.call-start
  8.7 1.3 convert_reduce_fusion
  10.0 42.5 %psum.7 = f32[]{:T(128)} all-reduce(f32[]{:T(128)} %convert_reduce_fusion), channel_id=1, replica_groups=mesh['row'=4,'col'=8] {'row','col'}, use_global_device_ids=true, to_apply=%region_6.0 | all-reduce | flops 1 | bytes 8 | tf_op jit(solution)/shard_map/psum | solution.py:49
  52.5 1.2 dynamic-slice
  54.4 0.9 dynamic-update-slice
  55.2 10.9 %all-reduce = s32[512]{0:T(512)S(1)} all-reduce(s32[512]{0:T(512)S(1)} %dynamic-update-slice), channel_id=1, replica_groups=mesh['row'=4,'col'=8] {'col'}, use_global_device_ids=true, to_apply=%add | all-reduce | flops 512 | bytes 4096
  66.2 7.7 %all_gather.12 = bf16[256,1024]{1,0:T(8,128)(2,1)S(1)} all-gather(bf16[64,1024]{1,0:T(8,128)(2,1)} %param.3), channel_id=1, replica_groups=mesh['row'=4,'col'=8] {'row'}, dimensions={0}, use_global_device_ids=true | all-gather | bytes 655360 | tf_op jit(solution)/shard_map/all_gather | solution.py:51
  73.9 0.2 fusion.12
  74.1 1.6 %multiply_reduce_fusion.1 = f32[512]{0:T(512)S(1)} fusion(bf16[512,1024]{1,0:T(8,128)(2,1)} %all-gather.3.cloned.1.call-done), kind=kLoop, calls=%fused_computation.1 | loop fusion | flops 1572352 | bytes 1050624 | tf_op jit(solution)/shard_map/reduce_sum | solution.py:9
  75.7 18.6 %all-gather.5.cloned.1.call-done = bf16[512,1024]{1,0:T(8,128)(2,1)} async-done(((bf16[64,1024]{1,0:T(8,128)(2,1)}), bf16[512,1024]{1,0:T(8,128)(2,1)}) %all-gather.5.cloned.1.call-update) | async-done | bytes 1048592 | tf_op jit(solution)/shard_map/all_gather | solution.py:66
  94.2 1.5 %multiply_reduce_fusion = f32[512]{0:T(512)S(1)} fusion(bf16[512,1024]{1,0:T(8,128)(2,1)} %all-gather.5.cloned.1.call-done), kind=kLoop, calls=%fused_computation | loop fusion | flops 1572352 | bytes 1050624 | tf_op jit(solution)/shard_map/reduce_sum | solution.py:9
  95.7 0.6 fusion.16
  96.4 0.4 fusion.2
  96.8 0.8 copy-done.1
  97.6 0.6 fusion.15
  98.2 2.1 %fusion.1 = f32[256,1024]{1,0:T(8,128)} fusion(f32[256,1024]{1,0:T(8,128)S(1)} %fusion.2, bf16[512,1024]{1,0:T(8,128)(2,1)S(1)} %copy-done.1, bf16[256,1024]{1,0:T(8,128)(2,1)S(1)} %all_gather.12, f32[]{:T(128)} %psum.7, f32[256]{0:T(256)S(1)} %get-tuple-element.2, bf16[256,512]{1,0:T(8,128)(2,1)S(1)} %get-tuple-element.3), kind=kOutput, calls=%fused_computation.7 | convolution fusion | flops 269746176 | bytes 3933188 | tf_op jit(solution)/shard_map/dot_general | solution.py:27
  100.3 0.6 copy-done.2
  100.9 0.6 dynamic-slice.1
  102.2 0.6 divide_subtract_fusion
  102.8 5.7 %all-reduce.1 = f32[256]{0:T(256)S(1)} all-reduce(f32[256]{0:T(256)S(1)} %divide_subtract_fusion), channel_id=2, replica_groups=mesh['row'=4,'col'=8] {'row'}, use_global_device_ids=true, to_apply=%region_7.0.clone | all-reduce | flops 256 | bytes 2048
  108.5 0.6 dynamic-slice.2
  109.0 14.9 %reduce-scatter.2.cloned.1.call-done = f32[64,1024]{1,0:T(8,128)} async-done(((f32[256,1024]{1,0:T(8,128)}), f32[64,1024]{1,0:T(8,128)}) %reduce-scatter.2.cloned.1.call-update) | async-done | bytes 262160 | tf_op jit(solution)/shard_map/reduce_scatter | solution.py:75
  (10 shorter events, 0.1 us)
Async XLA Ops:
  7.2 66.9 %all-gather.3.cloned.1.call-start = ((), (), s32[]{:S(2)}) async-start(), calls=%async_computation.1 | async-start | bytes 1179648 | tf_op jit(solution)/shard_map/all_gather | solution.py:68
  7.9 86.3 %all-gather.5.cloned.1.call-start = ((), (), s32[]{:S(2)}) async-start(), calls=%async_computation.2 | async-start | bytes 1179648 | tf_op jit(solution)/shard_map/all_gather | solution.py:66
  8.6 115.3 %reduce-scatter.2.cloned.1.call-start = ((), (), s32[]{:S(2)}) async-start(), calls=%async_computation.3 | async-start | bytes 1310720 | tf_op jit(solution)/shard_map/reduce_scatter | solution.py:75
  74.1 21.7 %copy-start = (bf16[512,1024]{1,0:T(8,128)(2,1)S(1)}, bf16[512,1024]{1,0:T(8,128)(2,1)}, u32[]{:S(2)}) copy-start(bf16[512,1024]{1,0:T(8,128)(2,1)} %all-gather.3.cloned.1.call-done) | copy-start | bytes 3145732
  96.4 1.2 copy-start.1
  100.3 0.7 copy-start.2
Sparse Core Ops, SparseCore 0:
  10.1 42.9 all-gather.2
  55.2 38.9 all-gather.4
  100.4 23.4 reduce-scatter.1
where the time goes:
time: 131 us; the launch traced here: 130 us
  blocking collectives  66.8 us (51%)
  waiting for transfers between devices  34.9 us (27%)
  between operations  15.1 us (12%)
  other arithmetic  5.16 us (4%)
  local copies, waits for them, and re-layouts  4.67 us (4%)
  matrix products  3.75 us (3%)
    psum x1, blocking collectives, on_device(): weight_total = lax.psum(jnp.sum(counts.astype(jnp.float32)), ('row', 'col'))  42.5 us
    all_gather x1, waiting for transfers between devices, on_device(): lax.all_gather(pool, 'col', axis=0, tiled=True)  18.6 us
    unnamed x2, blocking collectives  16.6 us
    reduce_scatter x1, waiting for transfers between devices, on_device(): lax.psum_scatter(gradient, 'row', scatter_dimension=0, tiled=True)  14.9 us
    all_gather x1, blocking collectives, on_device(): row_panel = lax.all_gather(pool, 'row', axis=0, tiled=True)  7.67 us
    unnamed x11, local copies, waits for them, and re-layouts  4.67 us
    reduce_sum x2, other arithmetic, kernel_tile(): col_norms = jnp.sum(col_float * col_float, axis=1)  3.09 us
  transfers between devices with their start and end apart: 3, of which 2 were waited for; matrix products, arithmetic and copies ran while one was open for 5% of the time, Pallas kernels for 0%

commit v1 on v0

v1 whole, which is shorter than its diff:
```python
import functools

import jax
import jax.numpy as jnp
from jax import lax
from jax.experimental import pallas as pl
from jax.experimental.pallas import tpu as pltpu
from jax.sharding import PartitionSpec as P

MESH = pl.DeviceIdType.MESH


def kernel(
    R, n, chunks,
    pool, targets, counts,
    g_out, p_out,
    rowbuf, colbuf, cnt, kp, kt, mp, mt, rn, acc, gbuf, pbuf, rs1, rp1, sbuf, spbuf, rs2, rp2,
    loc_sem, cnt_s, cnt_r, cnr_s, cnr_r, row_s, row_r, ring_s, ring_r,
    a_s, a_r, ap_s, ap_r, b_s, b_r, bp_s, bp_r,
):
    b, d = pool.shape
    half, pairs = n // 2, R // 2
    rows = R * b
    part = pairs * b
    dc = d // chunks
    target_count = b * R * n
    mr = lax.axis_index("row")
    mc = lax.axis_index("col")
    core = lax.rem(mr, 2)
    pair = lax.div(mr, 2)
    sibling = mr + 1 - 2 * core
    slot = core * pairs + pair

    def place(position):
        upper = lax.div(position, half)
        return 2 * (position + upper * (n - 1 - 2 * position)) + upper

    step_z = lax.div(mc, 2)
    step_y = lax.rem(mc, 2)
    pos = step_z + step_y * (n - 1 - 2 * step_z)

    def at_distance(k):
        return place(lax.rem(pos + k + n, n))

    neighbour = (at_distance(1), at_distance(-1))

    barrier = pltpu.get_barrier_semaphore()
    for k in range(1, n):
        pl.semaphore_signal(
            barrier, inc=1, device_id={"col": lax.rem(mc + k, n)}, device_id_type=MESH
        )
    for k in range(1, R):
        pl.semaphore_signal(
            barrier, inc=1, device_id={"row": lax.rem(mr + k, R)}, device_id_type=MESH
        )
    pl.semaphore_wait(barrier, n - 1 + R - 1)

    sent = []

    def send(src, dst, send_sem, recv_sem, device):
        copy = pltpu.make_async_remote_copy(
            src_ref=src, dst_ref=dst, send_sem=send_sem, recv_sem=recv_sem,
            device_id=device, device_id_type=MESH,
        )
        copy.start()
        sent.append(copy)
        return copy

    mine = (pool, targets)
    ring = {}

    def hop(s, way, t):
        src = mine[t] if s == 0 else colbuf.at[t, s - 1, way]
        dst = colbuf.at[t, s, 0 if s == half - 1 else way]
        ring[s, way, t] = send(
            src, dst, ring_s.at[s, way, t], ring_r.at[s, way, t], {"col": neighbour[way]}
        )

    count_copies = [
        send(
            counts, cnt.at[mr, mc], cnt_s.at[k], cnt_r.at[k], {"col": lax.rem(mc + k, n)}
        )
        for k in range(1, n)
    ]
    for t in range(2):
        for way in range(2):
            if half > 1 or way == t:
                hop(0, way, t)
    row_copies = [
        send(
            pool, rowbuf.at[slot], row_s.at[k], row_r.at[k], {"row": lax.rem(mr + k, R)}
        )
        for k in range(1, R)
    ]
    local = [
        pltpu.make_async_copy(counts, cnt.at[mr, mc], loc_sem.at[0]),
        pltpu.make_async_copy(pool, rowbuf.at[slot], loc_sem.at[1]),
        pltpu.make_async_copy(pool, colbuf.at[0, half - 1, 1], loc_sem.at[2]),
        pltpu.make_async_copy(targets, colbuf.at[1, half - 1, 1], loc_sem.at[3]),
    ]
    for copy in local:
        copy.start()
    local[0].wait()
    for copy in count_copies:
        copy.wait_recv()
    count_rows = [
        send(
            cnt.at[mr], cnt.at[mr], cnr_s.at[k], cnr_r.at[k], {"row": lax.rem(mr + k, R)}
        )
        for k in range(1, R)
    ]
    for copy in local[1:]:
        copy.wait()
    for copy in row_copies:
        copy.wait_recv()

    rc = min(rows, 256)
    per = rc // b

    def each_rows(body):
        if rows == rc:
            body(0)
        else:
            @pl.loop(0, rows // rc)
            def _(i):
                body(i)

    def span(i):
        return pl.ds(pl.multiple_of(i * rc, rc), rc)

    def panel(i):
        return rowbuf[pl.ds(i * per, per)].reshape(rc, d)

    def norms(i):
        x = panel(i).astype(jnp.float32)
        rn[span(i), :] = jnp.sum(x * x, axis=1, keepdims=True)
        mp[span(i), :] = jnp.zeros((rc, 2 * b), jnp.float32)
        mt[span(i), :] = jnp.zeros((rc, 2 * b), jnp.float32)

    each_rows(norms)

    for copy in count_rows:
        copy.wait_recv()
    all_counts = jnp.sum(cnt[...].astype(jnp.float32), axis=(0, 1))
    weight = 1.0 / jnp.sum(all_counts, axis=1, keepdims=True)
    share = 1.0 / target_count

    def tiles(s):
        x = jnp.concatenate([colbuf[t, s].reshape(2 * b, d) for t in range(2)], axis=0)
        xf = x.astype(jnp.float32)
        sums = jnp.sum(xf * xf, axis=1, keepdims=True)
        col_norms = jnp.broadcast_to(sums, (4 * b, 128)).T[0:1, :]
        first = at_distance(-(s + 1))
        second = mc if s == half - 1 else at_distance(s + 1)
        cw = jnp.concatenate([cnt[mr, first], cnt[mr, second]], axis=1).astype(jnp.float32)

        def body(i):
            inner = lax.dot_general(
                panel(i), x, (((1,), (1,)), ((), ())), preferred_element_type=jnp.float32
            )
            squared = rn[span(i), :] + col_norms - 2.0 * inner
            k = jnp.exp(-squared * (0.5 / d))
            pool_kernel = k[:, : 2 * b] * cw
            target_kernel = k[:, 2 * b :]
            mp[span(i), :] += pool_kernel
            mt[span(i), :] += target_kernel
            where = slice(s * 2 * b, (s + 1) * 2 * b)
            kp[span(i), where] = pool_kernel.astype(jnp.bfloat16)
            kt[span(i), where] = target_kernel.astype(jnp.bfloat16)

        each_rows(body)

    def pull(i, lo, hi, c):
        cols = slice(c * dc, (c + 1) * dc)
        inside = slice(lo * 2 * b, hi * 2 * b)
        p = jnp.dot(
            kp[span(i), inside],
            colbuf[0, lo:hi, :, :, cols].reshape((hi - lo) * 2 * b, dc),
            preferred_element_type=jnp.float32,
        )
        t = jnp.dot(
            kt[span(i), inside],
            colbuf[1, lo:hi, :, :, cols].reshape((hi - lo) * 2 * b, dc),
            preferred_element_type=jnp.float32,
        )
        return t * share - p * weight

    for s in range(half):
        for t in range(2):
            for way in range(2):
                if (s, way, t) in ring:
                    ring[s, way, t].wait_recv()
                    if s + 1 < half - 1 or (s + 1 == half - 1 and way == t):
                        hop(s + 1, way, t)
        if s == half - 1:
            break
        tiles(s)
        if s == half - 2:
            for c in range(chunks):
                def partial(i):
                    acc[c, span(i), :] = pull(i, 0, half - 1, c)

                each_rows(partial)
    tiles(half - 1)

    def masses(i):
        target_mass = jnp.sum(mt[span(i), :], axis=1, keepdims=True)
        pool_mass = jnp.sum(mp[span(i), :], axis=1, keepdims=True)
        proof = target_mass * share - pool_mass * weight
        rn[span(i), :] = proof

    each_rows(masses)
    proof_t = jnp.broadcast_to(rn[...], (rows, 128)).T[0:8, :]
    for r in range(R):
        pbuf[r] = proof_t[:, r * b : (r + 1) * b]

    other = 1 - core
    theirs = pl.ds(pl.multiple_of(other * part, part), part)
    own = pl.ds(pl.multiple_of(core * part, part), part)
    first_p = send(
        pbuf.at[pl.ds(other * pairs, pairs)], rp1, ap_s.at[0], ap_r.at[0], {"row": sibling}
    )
    first_g = []
    for c in range(chunks):
        def finish(i):
            cols = slice(c * dc, (c + 1) * dc)
            x = rowbuf[pl.ds(i * per, per), :, cols].reshape(rc, dc).astype(jnp.float32)
            grad = pull(i, half - 1, half, c) - rn[span(i), :] * x
            if half > 1:
                grad = grad + acc[c, span(i), :]
            gbuf[c, span(i), :] = grad

        each_rows(finish)
        first_g.append(
            send(gbuf.at[c, theirs], rs1.at[c], a_s.at[c], a_r.at[c], {"row": sibling})
        )

    first_p.wait_recv()
    spbuf[...] = pbuf[pl.ds(core * pairs, pairs)] + rp1[...]
    partners = [lax.rem(pair + k, pairs) for k in range(1, pairs)]
    second_p = [
        send(
            spbuf.at[partners[k]], rp2.at[k], bp_s.at[k], bp_r.at[k],
            {"row": 2 * partners[k] + core},
        )
        for k in range(pairs - 1)
    ]
    second_g = []
    for c in range(chunks):
        first_g[c].wait_recv()
        sbuf[c] = (gbuf[c, own, :] + rs1[c]).reshape(pairs, b, dc)
        for k in range(pairs - 1):
            second_g.append(
                send(
                    sbuf.at[c, partners[k]], rs2.at[c, k], b_s.at[c, k], b_r.at[c, k],
                    {"row": 2 * partners[k] + core},
                )
            )
    proof = spbuf[pair]
    for k in range(pairs - 1):
        second_p[k].wait_recv()
        proof = proof + rp2[k]
    p_out[...] = proof[0:1, :]
    for c in range(chunks):
        grad = sbuf[c, pair]
        for k in range(pairs - 1):
            second_g[c * (pairs - 1) + k].wait_recv()
            grad = grad + rs2[c, k]
        g_out[:, c * dc : (c + 1) * dc] = grad
    for copy in sent:
        copy.wait_send()


def on_device(R, n, pool, targets, counts):
    b, d = pool.shape
    half, pairs = n // 2, R // 2
    rows = R * b
    chunks = 4
    dc = d // chunks
    f32, bf16 = jnp.float32, jnp.bfloat16
    dma = pltpu.SemaphoreType.DMA
    far = max(pairs - 1, 1)
    vmem = pl.BlockSpec(memory_space=pltpu.VMEM)
    gradient, proof = pl.pallas_call(
        functools.partial(kernel, R, n, chunks),
        out_shape=(
            jax.ShapeDtypeStruct((b, d), f32),
            jax.ShapeDtypeStruct((1, b), f32),
        ),
        in_specs=[pl.BlockSpec(memory_space=pl.ANY)] * 2 + [vmem],
        out_specs=(vmem, vmem),
        scratch_shapes=[
            pltpu.VMEM((R, b, d), bf16),
            pltpu.VMEM((2, half, 2, b, d), bf16),
            pltpu.VMEM((R, n, 1, b), jnp.int32),
            pltpu.VMEM((rows, n * b), bf16),
            pltpu.VMEM((rows, n * b), bf16),
            pltpu.VMEM((rows, 2 * b), f32),
            pltpu.VMEM((rows, 2 * b), f32),
            pltpu.VMEM((rows, 1), f32),
            pltpu.VMEM((chunks, rows, dc), f32),
            pltpu.VMEM((chunks, rows, dc), f32),
            pltpu.VMEM((R, 8, b), f32),
            pltpu.VMEM((chunks, pairs * b, dc), f32),
            pltpu.VMEM((pairs, 8, b), f32),
            pltpu.VMEM((chunks, pairs, b, dc), f32),
            pltpu.VMEM((pairs, 8, b), f32),
            pltpu.VMEM((chunks, far, b, dc), f32),
            pltpu.VMEM((far, 8, b), f32),
            dma((4,)),
            dma((n,)), dma((n,)),
            dma((R,)), dma((R,)),
            dma((R,)), dma((R,)),
            dma((half, 2, 2)), dma((half, 2, 2)),
            dma((chunks,)), dma((chunks,)),
            dma((1,)), dma((1,)),
            dma((chunks, far)), dma((chunks, far)),
            dma((far,)), dma((far,)),
        ],
        compiler_params=pltpu.CompilerParams(collective_id=0, has_side_effects=True),
    )(pool, targets, counts.reshape(1, b))
    return proof.reshape(b), gradient


def solution(mesh):
    in_specs = (P(("row", "col"), None), P(("row", "col"), None), P(("row", "col")))
    out_specs = (P(("row", "col")), P(("row", "col"), None))
    return jax.shard_map(
        functools.partial(on_device, mesh.shape["row"], mesh.shape["col"]),
        mesh=mesh, in_specs=in_specs, out_specs=out_specs, check_vma=False,
    )
```

time: 131 us -> 47.1 us (0.36)
  blocking collectives: 66.8 us -> 0 us
  Pallas kernels: 0 us -> 43.5 us
  waiting for transfers between devices: 34.9 us -> 0 us
  between operations: 15.1 us -> 0.65 us
  other arithmetic: 5.16 us -> 0 us
  matrix products: 3.75 us -> 0 us
  local copies, waits for them, and re-layouts: 4.67 us -> 2.75 us
    pallas_call x0 -> x1, Pallas kernels: none -> 43.5 us  [on_device(): pl.pallas_call(functools.partial(kernel, R, n, chunks), out_shape=(jax.Sh...]
    psum x1 -> x0, blocking collectives: 42.5 us -> none  [on_device(): weight_total = lax.psum(jnp.sum(counts.astype(jnp.float32)), ('row', 'col'))]
    all_gather x2 -> x0, waiting for transfers between devices: 18.6 us -> none  [the longest x1 18.6 us: on_device(): lax.all_gather(pool, 'col', axis=0, tiled=True)]
    unnamed x2 -> x0, blocking collectives: 16.6 us -> none
    reduce_scatter x1 -> x0, waiting for transfers between devices: 14.9 us -> none  [on_device(): lax.psum_scatter(gradient, 'row', scatter_dimension=0, tiled=True)]
    all_gather x1 -> x0, blocking collectives: 7.67 us -> none  [on_device(): row_panel = lax.all_gather(pool, 'row', axis=0, tiled=True)]
    reduce_sum x4 -> x0, other arithmetic: 4.54 us -> none  [the longest x2 3.09 us: kernel_tile(): col_norms = jnp.sum(col_float * col_float, axis=1)]
    dot_general x4 -> x0, matrix products: 3.75 us -> none  [the longest x1 2.06 us: update(): jnp.dot(pool_kernel.astype(jnp.bfloat16), col_pool, preferred_element_typ...]
  transfers between devices with their start and end apart: 3 -> 0, of which waited for: 2 -> 0; matrix products, arithmetic and copies ran while one was open for 5% -> 0% of each run, Pallas kernels for 0% -> 0%
where the time goes in v1:
time: 47.1 us; the launch traced here: 46.9 us
  Pallas kernels  43.5 us (92%)
  local copies, waits for them, and re-layouts  2.75 us (6%)
  between operations  0.65 us (1%)
    pallas_call x1, Pallas kernels, on_device(): pl.pallas_call(functools.partial(kernel, R, n, chunks), out_shape=(jax.Sh...  43.5 us
    unnamed x4, local copies, waits for them, and re-layouts  2.75 us

profile of v1, /device:TPU:0, one launch (start us, length us, event | category | flops | bytes accessed | tf_op | source)
XLA Modules:
  0.0 46.9 jit_solution(9788365680299883778)
XLA Ops:
  0.6 43.5 %shard_map.50 = (f32[64,1024]{1,0:T(8,128)}, f32[1,64]{1,0:T(1,128)}) custom-call(bf16[64,1024]{1,0:T(8,128)(2,1)} %pool.1, bf16[64,1024]{1,0:T(8,128)(2,1)} %targets.1, s32[1,64]{1,0:T(1,128)} %bitcast.2), custom_call_target="tpu_custom_call" | custom-call | tf_op jit(solution)/shard_map/pallas_call | solution.py:284
  44.1 0.0 copy-start
  44.1 0.6 %copy-done = f32[1,64]{1,0:T(1,128)S(1)} copy-done((f32[1,64]{1,0:T(1,128)S(1)}, f32[1,64]{1,0:T(1,128)}, u32[]{:S(2)}) %copy-start) | copy-done | bytes 280
  44.7 0.5 %copy.7 = f32[64]{0:T(128)} copy(f32[64]{0:T(128)S(1)} %bitcast.3) | data formatting | bytes 512
  45.2 1.7 %copy.8 = f32[64,1024]{1,0:T(8,128)} copy(f32[64,1024]{1,0:T(8,128)} %get-tuple-element.9) | data formatting | bytes 524288
Async XLA Ops:
  44.1 0.6 %copy-start = (f32[1,64]{1,0:T(1,128)S(1)}, f32[1,64]{1,0:T(1,128)}, u32[]{:S(2)}) copy-start(f32[1,64]{1,0:T(1,128)} %get-tuple-element.4) | copy-start | bytes 772

commit v2 on v1

v2 whole, which is shorter than its diff:
```python
import functools

import jax
import jax.numpy as jnp
from jax import lax
from jax.experimental import pallas as pl
from jax.experimental.pallas import tpu as pltpu
from jax.sharding import PartitionSpec as P

MESH = pl.DeviceIdType.MESH


def kernel(
    R, n, chunks,
    pool, targets, counts,
    g_out, p_out, rs2, rp2,
    rowbuf, colbuf, cnt, kp, kt, mp, mt, rn, acc, gbuf, pbuf, rs1, rp1, own_g, sbuf, spbuf,
    loc_sem, cnt_s, cnt_r, cnr_s, cnr_r, row_s, row_r, ring_s, ring_r,
    a_s, a_r, ap_s, ap_r, b_s, b_r, bp_s, bp_r,
):
    b, d = pool.shape
    half, pairs = n // 2, R // 2
    rows = R * b
    part = pairs * b
    dc = d // chunks
    target_count = b * R * n
    mr = lax.axis_index("row")
    mc = lax.axis_index("col")
    core = lax.rem(mr, 2)
    pair = lax.div(mr, 2)
    sibling = mr + 1 - 2 * core
    slot = core * pairs + pair

    def place(position):
        upper = lax.div(position, half)
        return 2 * (position + upper * (n - 1 - 2 * position)) + upper

    step_z = lax.div(mc, 2)
    step_y = lax.rem(mc, 2)
    pos = step_z + step_y * (n - 1 - 2 * step_z)

    def at_distance(k):
        return place(lax.rem(pos + k + n, n))

    neighbour = (at_distance(1), at_distance(-1))

    barrier = pltpu.get_barrier_semaphore()
    for way in range(2):
        pl.semaphore_signal(
            barrier, inc=1, device_id={"col": neighbour[way]}, device_id_type=MESH
        )
    for k in range(1, R):
        pl.semaphore_signal(
            barrier, inc=1, device_id={"row": lax.rem(mr + k, R)}, device_id_type=MESH
        )
    pl.semaphore_wait(barrier, 2 + R - 1)

    sent = []

    def send(src, dst, send_sem, recv_sem, device):
        copy = pltpu.make_async_remote_copy(
            src_ref=src, dst_ref=dst, send_sem=send_sem, recv_sem=recv_sem,
            device_id=device, device_id_type=MESH,
        )
        copy.start()
        sent.append(copy)
        return copy

    mine = (pool, targets)
    ring = {}
    last = half - 1

    def slot_of(s, way):
        return n - 1 if s == last else 2 * s + way

    def hop(s, way, t):
        if s == last and way != t:
            return
        src = mine[t] if s == 0 else colbuf.at[t, slot_of(s - 1, way)]
        ring[s, way, t] = send(
            src, colbuf.at[t, slot_of(s, way)],
            ring_s.at[s, way, t], ring_r.at[s, way, t], {"col": neighbour[way]},
        )

    def count_hop(s, way):
        if s == last and way != 0:
            return
        owner = at_distance(-s if way == 0 else s)
        src = counts if s == 0 else cnt.at[mr, owner]
        ring[s, way, 2] = send(
            src, cnt.at[mr, owner],
            cnt_s.at[s, way], cnt_r.at[s, way], {"col": neighbour[way]},
        )

    for way in range(2):
        count_hop(0, way)
    for t in range(2):
        for way in range(2):
            hop(0, way, t)
    row_copies = [
        send(
            pool, rowbuf.at[slot], row_s.at[k], row_r.at[k], {"row": lax.rem(mr + k, R)}
        )
        for k in range(1, R)
    ]
    local = [
        pltpu.make_async_copy(counts, cnt.at[mr, mc], loc_sem.at[0]),
        pltpu.make_async_copy(pool, rowbuf.at[slot], loc_sem.at[1]),
        pltpu.make_async_copy(pool, colbuf.at[0, n - 2], loc_sem.at[2]),
        pltpu.make_async_copy(targets, colbuf.at[1, n - 2], loc_sem.at[3]),
    ]
    for copy in local:
        copy.start()

    def pass_counts(s):
        for way in range(2):
            if (s, way, 2) in ring:
                ring[s, way, 2].wait_recv()
                if s < last:
                    count_hop(s + 1, way)

    pass_counts(0)
    for copy in local:
        copy.wait()
    for copy in row_copies:
        copy.wait_recv()

    rc = min(rows, 256)
    per = rc // b

    def each_rows(body):
        if rows == rc:
            body(0)
        else:
            @pl.loop(0, rows // rc)
            def _(i):
                body(i)

    def span(i):
        return pl.ds(pl.multiple_of(i * rc, rc), rc)

    def panel(i):
        return rowbuf[pl.ds(i * per, per)].reshape(rc, d)

    def norms(i):
        x = panel(i).astype(jnp.float32)
        rn[span(i), :] = jnp.sum(x * x, axis=1, keepdims=True)
        mp[span(i), :] = jnp.zeros((rc, 2 * b), jnp.float32)
        mt[span(i), :] = jnp.zeros((rc, 2 * b), jnp.float32)

    each_rows(norms)

    def tiles(lo, owners, far=False):
        width = len(owners) * b
        x = jnp.concatenate(
            [colbuf[t, lo : lo + len(owners)].reshape(width, d) for t in range(2)], axis=0
        )
        xf = x.astype(jnp.float32)
        sums = jnp.sum(xf * xf, axis=1, keepdims=True)
        col_norms = jnp.broadcast_to(sums, (2 * width, 128)).T[0:1, :]
        cw = jnp.concatenate([cnt[mr, o] for o in owners], axis=1).astype(jnp.float32)

        def body(i):
            inner = lax.dot_general(
                panel(i), x, (((1,), (1,)), ((), ())), preferred_element_type=jnp.float32
            )
            squared = rn[span(i), :] + col_norms - 2.0 * inner
            k = jnp.exp(-squared * (0.5 / d))
            pool_kernel = k[:, :width] * cw
            target_kernel = k[:, width:]
            mp[span(i), :width] += pool_kernel
            mt[span(i), :width] += target_kernel
            where = slice(0, width) if far else slice(lo * b, lo * b + width)
            kp[span(i), where] = pool_kernel.astype(jnp.bfloat16)
            kt[span(i), where] = target_kernel.astype(jnp.bfloat16)

        each_rows(body)

    def pull(i, inside, lo, hi, c):
        cols = slice(c * dc, (c + 1) * dc)
        p = jnp.dot(
            kp[span(i), inside],
            colbuf[0, lo:hi, :, cols].reshape((hi - lo) * b, dc),
            preferred_element_type=jnp.float32,
        )
        t = jnp.dot(
            kt[span(i), inside],
            colbuf[1, lo:hi, :, cols].reshape((hi - lo) * b, dc),
            preferred_element_type=jnp.float32,
        )
        return t, p

    tiles(n - 2, [mc])
    share = 1.0 / target_count
    for s in range(last):
        if s > 0:
            pass_counts(s)
        for t in range(2):
            for way in range(2):
                ring[s, way, t].wait_recv()
                hop(s + 1, way, t)
        tiles(2 * s, [at_distance(-(s + 1)), at_distance(s + 1)])
    pass_counts(last)
    count_rows = [
        send(
            cnt.at[mr], cnt.at[mr], cnr_s.at[k], cnr_r.at[k], {"row": lax.rem(mr + k, R)}
        )
        for k in range(1, R)
    ]
    for copy in count_rows:
        copy.wait_recv()
    all_counts = jnp.sum(cnt[...].astype(jnp.float32), axis=(0, 1))
    weight = 1.0 / jnp.sum(all_counts, axis=1, keepdims=True)
    for c in range(chunks):
        def partial(i):
            t, p = pull(i, slice(0, (n - 1) * b), 0, n - 1, c)
            acc[c, span(i), :] = t * share - p * weight

        each_rows(partial)
    for t in range(2):
        ring[last, t, t].wait_recv()
    tiles(n - 1, [at_distance(half)], far=True)

    def masses(i):
        target_mass = jnp.sum(mt[span(i), :], axis=1, keepdims=True)
        pool_mass = jnp.sum(mp[span(i), :], axis=1, keepdims=True)
        proof = target_mass * share - pool_mass * weight
        rn[span(i), :] = proof

    each_rows(masses)
    proof_t = jnp.broadcast_to(rn[...], (rows, 128)).T[0:1, :]
    for r in range(R):
        pbuf[r] = proof_t[:, r * b : (r + 1) * b]

    other = 1 - core
    theirs = pl.ds(pl.multiple_of(other * part, part), part)
    first_p = send(
        pbuf.at[pl.ds(other * pairs, pairs)], rp1, ap_s.at[0], ap_r.at[0], {"row": sibling}
    )
    first_g = []
    for c in range(chunks):
        def finish(i):
            cols = slice(c * dc, (c + 1) * dc)
            x = rowbuf[pl.ds(i * per, per), :, cols].reshape(rc, dc).astype(jnp.float32)
            t, p = pull(i, slice(0, b), n - 1, n, c)
            gbuf[c, span(i), :] = acc[c, span(i), :] + (
                t * share - p * weight - rn[span(i), :] * x
            )

        each_rows(finish)
        first_g.append(
            send(gbuf.at[c, theirs], rs1.at[c], a_s.at[c], a_r.at[c], {"row": sibling})
        )

    first_p.wait_recv()
    spbuf[...] = pbuf[pl.ds(core * pairs, pairs)] + rp1[...]
    out_copies = [pltpu.make_async_copy(spbuf.at[pair], p_out, loc_sem.at[0])]
    out_copies[0].start()
    partners = [lax.rem(pair + k, pairs) for k in range(1, pairs)]
    arriving = [
        send(
            spbuf.at[partners[k]], rp2.at[k], bp_s.at[k], bp_r.at[k],
            {"row": 2 * partners[k] + core},
        )
        for k in range(pairs - 1)
    ]
    for c in range(chunks):
        cols = slice(c * dc, (c + 1) * dc)
        first_g[c].wait_recv()
        for k in range(pairs - 1):
            at = pl.multiple_of(partners[k] * b, b)
            block = gbuf[c, pl.ds(pl.multiple_of(core * part + at, b), b), :]
            sbuf[c, k] = (block + rs1[c, pl.ds(at, b), :]).astype(sbuf.dtype)
            arriving.append(
                send(
                    sbuf.at[c, k], rs2.at[k, :, cols], b_s.at[c, k], b_r.at[c, k],
                    {"row": 2 * partners[k] + core},
                )
            )
        at = pl.multiple_of(pair * b, b)
        block = gbuf[c, pl.ds(pl.multiple_of(core * part + at, b), b), :]
        own_g[:, cols] = block + rs1[c, pl.ds(at, b), :]
    out_copies.append(pltpu.make_async_copy(own_g, g_out, loc_sem.at[1]))
    out_copies[1].start()
    for copy in arriving:
        copy.wait_recv()
    for copy in sent:
        copy.wait_send()
    for copy in out_copies:
        copy.wait()


def on_device(R, n, pool, targets, counts):
    b, d = pool.shape
    half, pairs = n // 2, R // 2
    rows = R * b
    chunks = 4
    dc = d // chunks
    f32, bf16 = jnp.float32, jnp.bfloat16
    link = f32
    dma = pltpu.SemaphoreType.DMA
    far = pairs - 1
    hbm = pl.BlockSpec(memory_space=pl.ANY)
    own_g, own_p, far_g, far_p = pl.pallas_call(
        functools.partial(kernel, R, n, chunks),
        out_shape=(
            jax.ShapeDtypeStruct((b, d), f32),
            jax.ShapeDtypeStruct((1, b), f32),
            jax.ShapeDtypeStruct((far, b, d), link),
            jax.ShapeDtypeStruct((far, 1, b), f32),
        ),
        in_specs=[hbm, hbm, pl.BlockSpec(memory_space=pltpu.VMEM)],
        out_specs=(hbm, hbm, hbm, hbm),
        scratch_shapes=[
            pltpu.VMEM((R, b, d), bf16),
            pltpu.VMEM((2, n, b, d), bf16),
            pltpu.VMEM((R, n, 1, b), jnp.int32),
            pltpu.VMEM((rows, n * b), bf16),
            pltpu.VMEM((rows, n * b), bf16),
            pltpu.VMEM((rows, 2 * b), f32),
            pltpu.VMEM((rows, 2 * b), f32),
            pltpu.VMEM((rows, 1), f32),
            pltpu.VMEM((chunks, rows, dc), f32),
            pltpu.VMEM((chunks, rows, dc), f32),
            pltpu.VMEM((R, 1, b), f32),
            pltpu.VMEM((chunks, pairs * b, dc), f32),
            pltpu.VMEM((pairs, 1, b), f32),
            pltpu.VMEM((b, d), f32),
            pltpu.VMEM((chunks, far, b, dc), link),
            pltpu.VMEM((pairs, 1, b), f32),
            dma((4,)),
            dma((half, 2)), dma((half, 2)),
            dma((R,)), dma((R,)),
            dma((R,)), dma((R,)),
            dma((half, 2, 2)), dma((half, 2, 2)),
            dma((chunks,)), dma((chunks,)),
            dma((1,)), dma((1,)),
            dma((chunks, far)), dma((chunks, far)),
            dma((far,)), dma((far,)),
        ],
        compiler_params=pltpu.CompilerParams(collective_id=0, has_side_effects=True),
    )(pool, targets, counts.reshape(1, b))
    gradient = own_g
    proof = own_p.reshape(b)
    for k in range(far):
        gradient = gradient + far_g[k].astype(f32)
        proof = proof + far_p[k].reshape(b)
    return proof, gradient


def solution(mesh):
    in_specs = (P(("row", "col"), None), P(("row", "col"), None), P(("row", "col")))
    out_specs = (P(("row", "col")), P(("row", "col"), None))
    return jax.shard_map(
        functools.partial(on_device, mesh.shape["row"], mesh.shape["col"]),
        mesh=mesh, in_specs=in_specs, out_specs=out_specs, check_vma=False,
    )
```

time: 47.1 us -> 43.9 us (0.932)
  Pallas kernels: 43.5 us -> 40.2 us
  other arithmetic: 0 us -> 2.27 us
  local copies, waits for them, and re-layouts: 2.75 us -> 0.62 us
    pallas_call x1, Pallas kernels: 43.5 us -> 40.2 us  [on_device(): pl.pallas_call(functools.partial(kernel, R, n, chunks), out_shape=(jax.Sh...]
    add x0 -> x2, other arithmetic: none -> 2.27 us  [the longest x1 1.76 us: on_device(): gradient = gradient + far_g[k].astype(f32)]
    unnamed x4, local copies, waits for them, and re-layouts: 2.75 us -> 0.62 us
where the time goes in v2:
time: 43.9 us; the launch traced here: 43.7 us
  Pallas kernels  40.2 us (92%)
  other arithmetic  2.27 us (5%)
  between operations  0.66 us (2%)
  local copies, waits for them, and re-layouts  0.62 us (1%)
    pallas_call x1, Pallas kernels, on_device(): pl.pallas_call(functools.partial(kernel, R, n, chunks), out_shape=(jax.Sh...  40.2 us
    add x1, other arithmetic, on_device(): gradient = gradient + far_g[k].astype(f32)  1.76 us

profile of v2, /device:TPU:0, one launch (start us, length us, event | category | flops | bytes accessed | tf_op | source)
XLA Modules:
  0.0 43.7 jit_solution(5882594455311970839)
XLA Ops:
  0.6 40.2 %shard_map.50 = (f32[64,1024]{1,0:T(8,128)}, f32[1,64]{1,0:T(1,128)}, f32[1,64,1024]{2,1,0:T(8,128)}, f32[1,1,64]{2,1,0:T(1,128)}) custom-call(bf16[64,1024]{1,0:T(8,128)(2,1)} %pool.1, bf16[64,1024]{1,0:T(8,128)(2,1)} %targets.1, s32[1,64]{1,0:T(1,128)} %bitcast.7), custom_call_target="tpu_custom_call" | custom-call | tf_op jit(solution)/shard_map/pallas_call | solution.py:304
  40.8 0.0 copy-start
  40.8 0.0 copy-start.1
  40.8 0.6 %copy-done = f32[1,64]{1,0:T(1,128)S(1)} copy-done((f32[1,64]{1,0:T(1,128)S(1)}, f32[1,64]{1,0:T(1,128)}, u32[]{:S(2)}) %copy-start) | copy-done | bytes 280
  41.5 0.0 copy-done.1
  41.5 0.5 %bitcast_add_fusion.1 = f32[64]{0:T(128)} fusion(f32[1,1,64]{2,1,0:T(1,128)S(1)} %copy-done.1, f32[1,64]{1,0:T(1,128)S(1)} %copy-done), kind=kLoop, calls=%fused_computation.1 | loop fusion | flops 64 | bytes 768 | tf_op jit(solution)/shard_map/add | solution.py:347
  42.0 1.8 %bitcast_add_fusion = f32[64,1024]{1,0:T(8,128)} fusion(f32[64,1024]{1,0:T(8,128)} %get-tuple-element.8, f32[1,64,1024]{2,1,0:T(8,128)} %get-tuple-element.9), kind=kLoop, calls=%fused_computation | loop fusion | flops 65536 | bytes 786432 | tf_op jit(solution)/shard_map/add | solution.py:346
Async XLA Ops:
  40.8 0.6 %copy-start = (f32[1,64]{1,0:T(1,128)S(1)}, f32[1,64]{1,0:T(1,128)}, u32[]{:S(2)}) copy-start(f32[1,64]{1,0:T(1,128)} %get-tuple-element.6) | copy-start | bytes 772
  40.8 0.6 %copy-start.1 = (f32[1,1,64]{2,1,0:T(1,128)S(1)}, f32[1,1,64]{2,1,0:T(1,128)}, u32[]{:S(2)}) copy-start(f32[1,1,64]{2,1,0:T(1,128)} %get-tuple-element.7) | copy-start | bytes 772

commit v3 on v2

--- a/solution.py
+++ b/solution.py
@@ -94,9 +94,8 @@
 
     for way in range(2):
         count_hop(0, way)
-    for t in range(2):
-        for way in range(2):
-            hop(0, way, t)
+    for way in range(2):
+        hop(0, way, 0)
     row_copies = [
         send(
             pool, rowbuf.at[slot], row_s.at[k], row_r.at[k], {"row": lax.rem(mr + k, R)}
@@ -119,6 +118,11 @@
                 if s < last:
                     count_hop(s + 1, way)
 
+    for way in range(2):
+        ring[0, way, 0].wait_send()
+        sent[:] = [c for c in sent if c is not ring[0, way, 0]]
+    for way in range(2):
+        hop(0, way, 1)
     pass_counts(0)
     for copy in local:
         copy.wait()
@@ -309,7 +313,7 @@
             jax.ShapeDtypeStruct((far, b, d), link),
             jax.ShapeDtypeStruct((far, 1, b), f32),
         ),
-        in_specs=[hbm, hbm, pl.BlockSpec(memory_space=pltpu.VMEM)],
+        in_specs=[pl.BlockSpec(memory_space=pltpu.HBM)] * 2 + [pl.BlockSpec(memory_space=pltpu.VMEM)],
         out_specs=(hbm, hbm, hbm, hbm),
         scratch_shapes=[
             pltpu.VMEM((R, b, d), bf16),
@@ -338,7 +342,7 @@
             dma((chunks, far)), dma((chunks, far)),
             dma((far,)), dma((far,)),
         ],
-        compiler_params=pltpu.CompilerParams(collective_id=0, has_side_effects=True),
+        compiler_params=pltpu.CompilerParams(vmem_limit_bytes=(16 << 20) + 32 * rows * d, collective_id=0, has_side_effects=True),
     )(pool, targets, counts.reshape(1, b))
     gradient = own_g
     proof = own_p.reshape(b)

time: 43.9 us -> 43.6 us (level)
  local copies, waits for them, and re-layouts: 0.62 us -> 2.46 us
  Pallas kernels: 40.2 us -> 39 us
  other arithmetic: 2.27 us -> 1.26 us
    unnamed x4 -> x6, local copies, waits for them, and re-layouts: 0.62 us -> 2.46 us
    pallas_call x1, Pallas kernels: 40.2 us -> 39 us  [on_device(): pl.pallas_call(functools.partial(kernel, R, n, chunks), out_shape=(jax.Sh...]
    add x1, other arithmetic: 1.76 us -> 0.74 us  [on_device(): gradient = gradient + far_g[k].astype(f32)]
where the time goes in v3:
time: 43.6 us; the launch traced here: 43.4 us
  Pallas kernels  39 us (89%)
  local copies, waits for them, and re-layouts  2.46 us (6%)
  other arithmetic  1.26 us (3%)
  between operations  0.65 us (1%)
    pallas_call x1, Pallas kernels, on_device(): pl.pallas_call(functools.partial(kernel, R, n, chunks), out_shape=(jax.Sh...  39 us
    unnamed x6, local copies, waits for them, and re-layouts  2.46 us

profile of v3, /device:TPU:0, one launch (start us, length us, event | category | flops | bytes accessed | tf_op | source)
XLA Modules:
  0.0 43.4 jit_solution(9721458859917385987)
XLA Ops:
  0.6 0.0 copy-start.2
  0.6 0.6 %copy-done.2 = s32[64]{0:T(128)S(1)} copy-done((s32[64]{0:T(128)S(1)}, s32[64]{0:T(128)}, u32[]{:S(2)}) %copy-start.2) | copy-done | bytes 280
  1.3 0.0 copy-start
  1.3 0.9 %copy-done = bf16[64,1024]{1,0:T(8,128)(2,1)S(1)} copy-done((bf16[64,1024]{1,0:T(8,128)(2,1)S(1)}, bf16[64,1024]{1,0:T(8,128)(2,1)}, u32[]{:S(2)}) %copy-start) | copy-done | bytes 131096
  2.2 0.0 copy-start.1
  2.2 0.9 %copy-done.1 = bf16[64,1024]{1,0:T(8,128)(2,1)S(1)} copy-done((bf16[64,1024]{1,0:T(8,128)(2,1)S(1)}, bf16[64,1024]{1,0:T(8,128)(2,1)}, u32[]{:S(2)}) %copy-start.1) | copy-done | bytes 131096
  3.1 39.0 %shard_map.50 = (f32[64,1024]{1,0:T(8,128)S(1)}, f32[1,64]{1,0:T(1,128)S(1)}, f32[1,64,1024]{2,1,0:T(8,128)S(1)}, f32[1,1,64]{2,1,0:T(1,128)S(1)}) custom-call(bf16[64,1024]{1,0:T(8,128)(2,1)S(1)} %copy-done, bf16[64,1024]{1,0:T(8,128)(2,1)S(1)} %copy-done.1, s32[1,64]{1,0:T(1,128)S(1)} %bitcast.7), custom_call_target="tpu_custom_call" | custom-call | tf_op jit(solution)/shard_map/pallas_call | solution.py:308
  42.1 0.5 %bitcast_add_fusion.1 = f32[64]{0:T(128)} fusion(f32[1,1,64]{2,1,0:T(1,128)S(1)} %get-tuple-element.7, f32[1,64]{1,0:T(1,128)S(1)} %get-tuple-element.6), kind=kLoop, calls=%fused_computation.1 | loop fusion | flops 64 | bytes 768 | tf_op jit(solution)/shard_map/add | solution.py:351
  42.7 0.7 %bitcast_add_fusion = f32[64,1024]{1,0:T(8,128)} fusion(f32[64,1024]{1,0:T(8,128)S(1)} %get-tuple-element.8, f32[1,64,1024]{2,1,0:T(8,128)S(1)} %get-tuple-element.9), kind=kLoop, calls=%fused_computation | loop fusion | flops 65536 | bytes 786432 | tf_op jit(solution)/shard_map/add | solution.py:350
Async XLA Ops:
  0.6 0.7 %copy-start.2 = (s32[64]{0:T(128)S(1)}, s32[64]{0:T(128)}, u32[]{:S(2)}) copy-start(s32[64]{0:T(128)} %param.5) | copy-start | bytes 772
  1.3 0.9 %copy-start = (bf16[64,1024]{1,0:T(8,128)(2,1)S(1)}, bf16[64,1024]{1,0:T(8,128)(2,1)}, u32[]{:S(2)}) copy-start(bf16[64,1024]{1,0:T(8,128)(2,1)} %pool.1) | copy-start | bytes 393220
  2.2 0.9 %copy-start.1 = (bf16[64,1024]{1,0:T(8,128)(2,1)S(1)}, bf16[64,1024]{1,0:T(8,128)(2,1)}, u32[]{:S(2)}) copy-start(bf16[64,1024]{1,0:T(8,128)(2,1)} %targets.1) | copy-start | bytes 393220
